TPU v7x, 256 devices: a whole 4x4x8 slice. The times are simulated.
256 devices in a mesh: row: 32 (over z, y), col: 8 (over x, core).
Axes of the slice: x: 4, y: 4, z: 8, core: 2. Of those that a mesh axis runs over, the one named last changes fastest.
Arguments:
- expression: bfloat16 [32768, 1024], P(('row', 'col')), as said below
- power_order: int32 [20], replicated, may hold values from 0 to 19, each once
Outputs:
- log_conn: float32 [32768, 20], P(('row', 'col'))
- fit: float32 [20], replicated
- slope: float32 [20], replicated
Inputs may be any that keep to these rules, and one draw needn't show every extreme that they name: `expression`: each gene's row has mean zero and unit variance over the samples, up to rounding.
All inputs are finite; a program needn't handle non-finite values.
Results may differ from a plain program's by a relative error of at most 0.0029.
Values may be sent and summed in bfloat16 or wider, within the bound.
A program may use at most 64 MiB of HBM per device.

v0:
```python
import functools
import math
import jax
import jax.numpy as jnp
from jax import lax
from jax.sharding import Mesh
from jax.sharding import PartitionSpec as P

ROW = ("row_0", "row_1")
COL = ("col_0", "col_1")
ROW_COL = ("row_0", "row_1", "col_0", "col_1")


def from_everyone(x, axis):
    copies = jnp.broadcast_to(x, (lax.axis_size(axis), *x.shape))
    return lax.all_to_all(copies, axis, split_axis=0, concat_axis=0, tiled=True)


def in_order(tiles, dim):
    tiles = jnp.moveaxis(tiles, 0, dim)
    lengths = tiles.shape
    return tiles.reshape(*lengths[:dim], lengths[dim] * lengths[dim + 1], *lengths[dim + 2 :])


def gather_directly(x, axis, dim):
    tiles = from_everyone(x, axis)
    return in_order(tiles, dim)


def cut_along(x, dim, devices):
    lengths = x.shape
    tiles = x.reshape(*lengths[:dim], devices, lengths[dim] // devices, *lengths[dim + 1 :])
    return jnp.moveaxis(tiles, dim, 0)


def sum_at_owner(x, axis, dim):
    tiles = cut_along(x, dim, lax.axis_size(axis))
    arrived = lax.all_to_all(tiles, axis, split_axis=0, concat_axis=0, tiled=True)
    return arrived.sum(axis=0)


def over_axes(x, axes):
    return functools.reduce(lax.psum, axes, x)


def power_sums(rows, partners, samples, powers):
    corr = (
        lax.dot_general(
            rows, partners, (((1,), (1,)), ((), ())), preferred_element_type=jnp.float32
        )
        / samples
    )
    magnitude = jnp.abs(corr)
    current = magnitude
    sums = []
    for power in range(powers):
        sums.append(jnp.sum(current, axis=1))
        current = current * magnitude
    return jnp.stack(sums, axis=1)


def scale_free_fit(hist, log_total, bins):
    centers = jnp.arange(bins, dtype=jnp.float32) * (log_total / (bins - 1))
    weight_sum = jnp.sum(hist, axis=1, keepdims=True)
    ylog = jnp.log(hist + 1.0) - log_total
    xmean = jnp.sum(hist * centers[None, :], axis=1, keepdims=True) / weight_sum
    ymean = jnp.sum(hist * ylog, axis=1, keepdims=True) / weight_sum
    xdev = centers[None, :] - xmean
    ydev = ylog - ymean
    sxx = jnp.maximum(jnp.sum(hist * xdev * xdev, axis=1) / weight_sum[:, 0], 0.05)
    syy = jnp.maximum(jnp.sum(hist * ydev * ydev, axis=1) / weight_sum[:, 0], 0.05)
    sxy = jnp.sum(hist * xdev * ydev, axis=1) / weight_sum[:, 0]
    return (-sxy * jnp.abs(sxy) / (sxx * syy), sxy / sxx)


def on_device(expression, power_order):
    samples = expression.shape[1]
    powers = power_order.shape[0]
    bins = 128
    genes_total = expression.shape[0] * lax.axis_size(ROW) * lax.axis_size(COL)
    panel = gather_directly(expression, COL, 0)
    partial_value = power_sums(
        panel, lax.all_gather(expression, ROW, axis=0, tiled=True), samples, powers
    )
    conn = sum_at_owner(partial_value, COL, 0)
    selector = (power_order[:, None] == jnp.arange(powers, dtype=jnp.int32)[None, :]).astype(
        jnp.float32
    )
    picked = jnp.dot(conn, selector.T, precision=lax.Precision.HIGHEST)
    log_conn = jnp.log(picked)
    log_total = math.log(genes_total)
    position = log_conn * ((bins - 1) / log_total)
    levels = jnp.arange(bins, dtype=jnp.float32)
    weights = jnp.maximum(0.0, 1.0 - jnp.abs(position[:, :, None] - levels[None, None, :]))
    local_hist = jnp.sum(weights, axis=0)
    hist = over_axes(local_hist, ROW_COL)
    fit, slope = scale_free_fit(hist, log_total, bins)
    return (log_conn, fit, slope)


def solution(mesh):
    torus = Mesh(mesh.devices.reshape(8, 4, 4, 2), ("row_0", "row_1", "col_0", "col_1"))
    return jax.shard_map(
        on_device,
        mesh=torus,
        in_specs=(P(ROW_COL, None), P()),
        out_specs=(P(ROW_COL, None), P(), P()),
        check_vma=False,
    )
```

profile of v0, /device:TPU:1, one launch (start us, length us, event | category | flops | bytes accessed | tf_op | source)
XLA Modules:
  0.0 238.8 jit_solution(6960383103107341380)
XLA Ops:
  7.2 0.0 all-gather.2.cloned.1.call-start
  7.2 0.7 all-gather.2.cloned.1.call-update
  7.9 1.2 broadcast_in_dim.2
  9.1 31.9 %all_to_all.10 = bf16[8,128,1024]{2,1,0:T(8,128)(2,1)S(1)} all-to-all(bf16[8,128,1024]{2,1,0:T(8,128)(2,1)S(1)} %broadcast_in_dim.2), channel_id=1, replica_groups=mesh['row_0'=8,'row_1'=4,'col_0'=4,'col_1'=2] {'col_0','col_1'}, dimensions={0} | all-to-all | bytes 4194304 | tf_op jit(solution)/shard_map/all_to_all | solution.py:16
  41.0 70.6 %all-gather.2.cloned.1.call-done = bf16[4096,1024]{1,0:T(8,128)(2,1)} async-done(((bf16[128,1024]{1,0:T(8,128)(2,1)}), bf16[4096,1024]{1,0:T(8,128)(2,1)}) %all-gather.2.cloned.1.call-update) | async-done | bytes 8388624 | tf_op jit(solution)/shard_map/all_gather | solution.py:83
  111.5 0.0 copy-start
  111.5 43.9 %multiply_reduce_fusion = (f32[1024]{0:T(1024)S(1)}, f32[1024]{0:T(1024)S(1)}, f32[1024]{0:T(1024)S(1)}, f32[1024]{0:T(1024)S(1)}, f32[1024]{0:T(1024)S(1)}, /*i...) fusion(bf16[1024,1024]{1,0:T(8,128)(2,1)S(1)} %bitcast.44, ...), kind=kOutput, calls=%fused_computation | convolution fusion | flops 8761880576 | bytes 10567680 | tf_op jit(solution)/shard_map/dot_general | solution.py:48
  155.6 0.6 copy.10
  156.3 5.7 %all-to-all-start.1 = ((f32[8,128,20]{1,2,0:T(8,128)}), f32[8,128,20]{1,2,0:T(8,128)S(1)}, u32[]{:S(2)}, u32[]{:S(2)}) async-start(f32[8,128,20]{1,2,0:T(8,128)} %copy.10), calls=%async_computation.1 | async-start | bytes 196608 | tf_op jit(solution)/shard_map/all_to_all | solution.py:38
  161.9 5.0 %all-to-all-done.1 = f32[8,128,20]{1,2,0:T(8,128)S(1)} async-done(((f32[8,128,20]{1,2,0:T(8,128)}), f32[8,128,20]{1,2,0:T(8,128)S(1)}, u32[]{:S(2)}, u32[]{:S(2)}) %all-to-all-start.1) | async-done | bytes 81952 | tf_op jit(solution)/shard_map/all_to_all | solution.py:38
  166.9 0.0 copy-done
  166.9 0.8 broadcast_multiply_fusion
  167.7 0.4 maximum_reduce_fusion
  168.2 21.0 %psum.28 = f32[20,128]{1,0:T(8,128)S(1)} all-reduce(f32[20,128]{1,0:T(8,128)S(1)} %maximum_reduce_fusion), channel_id=1, replica_groups=mesh['row_0'=8,'row_1'=4,'col_0'=4,'col_1'=2] {'row_0'}, use_global_device_ids=true, to_apply=%region_22.0 | all-reduce | flops 2560 | bytes 20480 | tf_op jit(solution)/shard_map/psum | solution.py:43
  189.2 11.2 %psum.29 = f32[20,128]{1,0:T(8,128)S(1)} all-reduce(f32[20,128]{1,0:T(8,128)S(1)} %psum.28), channel_id=1, replica_groups=mesh['row_0'=8,'row_1'=4,'col_0'=4,'col_1'=2] {'row_1'}, use_global_device_ids=true, to_apply=%region_23.0 | all-reduce | flops 2560 | bytes 20480 | tf_op jit(solution)/shard_map/psum | solution.py:43
  200.3 11.6 %psum.30 = f32[20,128]{1,0:T(8,128)S(1)} all-reduce(f32[20,128]{1,0:T(8,128)S(1)} %psum.29), channel_id=1, replica_groups=mesh['row_0'=8,'row_1'=4,'col_0'=4,'col_1'=2] {'col_0'}, use_global_device_ids=true, to_apply=%region_24.0 | all-reduce | flops 2560 | bytes 20480 | tf_op jit(solution)/shard_map/psum | solution.py:43
  211.9 18.6 %psum.31 = f32[20,128]{1,0:T(8,128)S(1)} all-reduce(f32[20,128]{1,0:T(8,128)S(1)} %psum.30), channel_id=1, replica_groups=mesh['row_0'=8,'row_1'=4,'col_0'=4,'col_1'=2] {'col_1'}, use_global_device_ids=true, to_apply=%region_25.0 | all-reduce | flops 2560 | bytes 20480 | tf_op jit(solution)/shard_map/psum | solution.py:43
  230.5 0.2 multiply_reduce_fusion.11
  230.7 0.2 multiply_reduce_fusion.10
  230.9 0.5 multiply_divide_fusion
  231.4 0.5 multiply_divide_fusion.1
  (23 shorter events, 0.1 us)
Async XLA Ops:
  7.2 104.4 %all-gather.2.cloned.1.call-start = ((), (), s32[]{:S(2)}) async-start(), calls=%async_computation.2 | async-start | bytes 8650752 | tf_op jit(solution)/shard_map/all_gather | solution.py:83
  111.5 55.4 %copy-start = (s32[20]{0:T(128)S(1)}, s32[20]{0:T(128)}, u32[]{:S(2)}) copy-start(s32[20]{0:T(128)} %param.3) | copy-start | bytes 244
  156.3 10.6 %all-to-all-start.1 = ((f32[8,128,20]{1,2,0:T(8,128)}), f32[8,128,20]{1,2,0:T(8,128)S(1)}, u32[]{:S(2)}, u32[]{:S(2)}) async-start(f32[8,128,20]{1,2,0:T(8,128)} %copy.10), calls=%async_computation.1 | async-start | bytes 196608 | tf_op jit(solution)/shard_map/all_to_all | solution.py:38
Sparse Core Ops, SparseCore 0:
  10.6 100.9 all-gather.1
where the time goes:
time: 239 us
  blocking collectives  94.2 us (39%)
  waiting for transfers between devices  76.2 us (32%)
  matrix products  44.7 us (19%)
  between operations  14.2 us (6%)
  starting transfers between devices  5.69 us (2%)
    all_gather x1, waiting for transfers between devices, on_device(): lax.all_gather(expression, ROW, axis=0, tiled=True)  70.6 us
    psum x4, blocking collectives, over_axes(): return functools.reduce(lax.psum, axes, x)  62.3 us
    dot_general x1, matrix products, power_sums(): lax.dot_general(rows, partners, (((1,), (1,)), ((), ())), preferred_eleme...  43.9 us
    all_to_all x1, blocking collectives, from_everyone(): return lax.all_to_all(copies, axis, split_axis=0, concat_axis=0, tiled=True)  31.9 us
    all_to_all x1, starting transfers between devices, sum_at_owner(): lax.all_to_all(tiles, axis, split_axis=0, concat_axis=0, tiled=True)  5.66 us
    all_to_all x1, waiting for transfers between devices, sum_at_owner(): lax.all_to_all(tiles, axis, split_axis=0, concat_axis=0, tiled=True)  4.97 us
  transfers between devices with their start and end apart: 2, of which 2 were waited for; matrix products, arithmetic and copies ran while one was open for 1% of the time, Pallas kernels for 0%

commit v1 on v0

--- a/solution.py
+++ b/solution.py
@@ -79,9 +79,19 @@
     bins = 128
     genes_total = expression.shape[0] * lax.axis_size(ROW) * lax.axis_size(COL)
     panel = gather_directly(expression, COL, 0)
-    partial_value = power_sums(
-        panel, lax.all_gather(expression, ROW, axis=0, tiled=True), samples, powers
-    )
+
+    def _get_notes(patch, lane_axis):
+        return jnp.concatenate(
+            lax.all_to_all(
+                jnp.stack([patch for _ in range(lax.axis_size(lane_axis))]),
+                concat_axis=0,
+                axis_name=lane_axis,
+                split_axis=0,
+            ),
+            axis=0,
+        )
+
+    partial_value = power_sums(panel, _get_notes(expression, ROW), samples, powers)
     conn = sum_at_owner(partial_value, COL, 0)
     selector = (power_order[:, None] == jnp.arange(powers, dtype=jnp.int32)[None, :]).astype(
         jnp.float32

time: 239 us -> 372 us (1.56)
  blocking collectives: 94.2 us -> 290 us
  waiting for transfers between devices: 76.2 us -> 4.99 us
  matrix products: 44.7 us -> 63.8 us
  between operations: 14.2 us -> 0.84 us
    all_to_all x0 -> x1, blocking collectives: none -> 194 us  [_get_notes(): lax.all_to_all(jnp.stack([patch for _ in range(lax.axis_size(lane_axis))]...]
    all_gather x1 -> x0, waiting for transfers between devices: 70.6 us -> none  [on_device(): lax.all_gather(expression, ROW, axis=0, tiled=True)]
    dot_general x1, matrix products: 43.9 us -> 63 us  [power_sums(): lax.dot_general(rows, partners, (((1,), (1,)), ((), ())), preferred_eleme...]
  transfers between devices with their start and end apart: 2 -> 1, of which waited for: 2 -> 1; matrix products, arithmetic and copies ran while one was open for 1% -> 0% of each run, Pallas kernels for 0% -> 0%
where the time goes in v1:
time: 372 us
  blocking collectives  290 us (78%)
  matrix products  63.8 us (17%)
  starting transfers between devices  6.28 us (2%)
  waiting for transfers between devices  4.99 us (1%)
  local copies, waits for them, and re-layouts  3.92 us (1%)
    all_to_all x1, blocking collectives, _get_notes(): lax.all_to_all(jnp.stack([patch for _ in range(lax.axis_size(lane_axis))]...  194 us
    psum x4, blocking collectives, over_axes(): return functools.reduce(lax.psum, axes, x)  63.8 us
    dot_general x1, matrix products, power_sums(): lax.dot_general(rows, partners, (((1,), (1,)), ((), ())), preferred_eleme...  63 us
    all_to_all x1, blocking collectives, from_everyone(): return lax.all_to_all(copies, axis, split_axis=0, concat_axis=0, tiled=True)  31.8 us
  transfers between devices with their start and end apart: 1, of which 1 were waited for; matrix products, arithmetic and copies ran while one was open for 0% of the time, Pallas kernels for 0%

profile of v1, /device:TPU:1, one launch (start us, length us, event | category | flops | bytes accessed | tf_op | source)
XLA Modules:
  0.0 371.5 jit_solution(13709309349299670378)
XLA Ops:
  0.6 1.2 broadcast_in_dim.2
  1.8 31.8 %all_to_all.15 = bf16[8,128,1024]{2,1,0:T(8,128)(2,1)S(1)} all-to-all(bf16[8,128,1024]{2,1,0:T(8,128)(2,1)S(1)} %broadcast_in_dim.2), channel_id=1, replica_groups=mesh['row_0'=8,'row_1'=4,'col_0'=4,'col_1'=2] {'col_0','col_1'}, dimensions={0} | all-to-all | bytes 4194304 | tf_op jit(solution)/shard_map/all_to_all | solution.py:16
  33.7 2.0 stack.44
  35.7 194.2 %all_to_all.16 = bf16[32,128,1024]{2,1,0:T(8,128)(2,1)S(1)} all-to-all(bf16[32,128,1024]{2,1,0:T(8,128)(2,1)S(1)} %stack.44), channel_id=1, replica_groups=mesh['row_0'=8,'row_1'=4,'col_0'=4,'col_1'=2] {'row_0','row_1'}, dimensions={0} | all-to-all | bytes 16777216 | tf_op jit(solution)/shard_map/all_to_all | solution.py:85
  229.9 0.0 copy-start
  229.9 63.0 %multiply_reduce_fusion = (f32[1024]{0:T(1024)S(1)}, f32[1024]{0:T(1024)S(1)}, f32[1024]{0:T(1024)S(1)}, f32[1024]{0:T(1024)S(1)}, f32[1024]{0:T(1024)S(1)}, /*i...) fusion(bf16[1024,1024]{1,0:T(8,128)(2,1)S(1)} %bitcast.46, ...), kind=kOutput, calls=%fused_computation | convolution fusion | flops 8761880576 | bytes 10567680 | tf_op jit(solution)/shard_map/dot_general | solution.py:48
  293.1 0.6 copy.10
  293.8 6.3 %all-to-all-start.2 = ((f32[8,128,20]{1,2,0:T(8,128)}), f32[8,128,20]{1,2,0:T(8,128)S(1)}, u32[]{:S(2)}, u32[]{:S(2)}) async-start(f32[8,128,20]{1,2,0:T(8,128)} %copy.10), calls=%async_computation.2 | async-start | bytes 196608 | tf_op jit(solution)/shard_map/all_to_all | solution.py:38
  300.1 5.0 %all-to-all-done.2 = f32[8,128,20]{1,2,0:T(8,128)S(1)} async-done(((f32[8,128,20]{1,2,0:T(8,128)}), f32[8,128,20]{1,2,0:T(8,128)S(1)}, u32[]{:S(2)}, u32[]{:S(2)}) %all-to-all-start.2) | async-done | bytes 81952 | tf_op jit(solution)/shard_map/all_to_all | solution.py:38
  305.1 0.0 copy-done
  305.1 0.8 broadcast_multiply_fusion
  305.9 0.4 maximum_reduce_fusion
  306.3 20.6 %psum.28 = f32[20,128]{1,0:T(8,128)S(1)} all-reduce(f32[20,128]{1,0:T(8,128)S(1)} %maximum_reduce_fusion), channel_id=1, replica_groups=mesh['row_0'=8,'row_1'=4,'col_0'=4,'col_1'=2] {'row_0'}, use_global_device_ids=true, to_apply=%region_22.0 | all-reduce | flops 2560 | bytes 20480 | tf_op jit(solution)/shard_map/psum | solution.py:43
  326.9 13.4 %psum.29 = f32[20,128]{1,0:T(8,128)S(1)} all-reduce(f32[20,128]{1,0:T(8,128)S(1)} %psum.28), channel_id=1, replica_groups=mesh['row_0'=8,'row_1'=4,'col_0'=4,'col_1'=2] {'row_1'}, use_global_device_ids=true, to_apply=%region_23.0 | all-reduce | flops 2560 | bytes 20480 | tf_op jit(solution)/shard_map/psum | solution.py:43
  340.3 11.5 %psum.30 = f32[20,128]{1,0:T(8,128)S(1)} all-reduce(f32[20,128]{1,0:T(8,128)S(1)} %psum.29), channel_id=1, replica_groups=mesh['row_0'=8,'row_1'=4,'col_0'=4,'col_1'=2] {'col_0'}, use_global_device_ids=true, to_apply=%region_24.0 | all-reduce | flops 2560 | bytes 20480 | tf_op jit(solution)/shard_map/psum | solution.py:43
  351.8 18.3 %psum.31 = f32[20,128]{1,0:T(8,128)S(1)} all-reduce(f32[20,128]{1,0:T(8,128)S(1)} %psum.30), channel_id=1, replica_groups=mesh['row_0'=8,'row_1'=4,'col_0'=4,'col_1'=2] {'col_1'}, use_global_device_ids=true, to_apply=%region_25.0 | all-reduce | flops 2560 | bytes 20480 | tf_op jit(solution)/shard_map/psum | solution.py:43
  370.1 0.2 multiply_reduce_fusion.11
  370.3 0.2 multiply_reduce_fusion.10
  370.5 0.5 multiply_divide_fusion
  371.0 0.5 multiply_divide_fusion.1
  (23 shorter events, 0.1 us)
Async XLA Ops:
  229.9 75.2 %copy-start = (s32[20]{0:T(128)S(1)}, s32[20]{0:T(128)}, u32[]{:S(2)}) copy-start(s32[20]{0:T(128)} %param.3) | copy-start | bytes 244
  293.8 11.3 %all-to-all-start.2 = ((f32[8,128,20]{1,2,0:T(8,128)}), f32[8,128,20]{1,2,0:T(8,128)S(1)}, u32[]{:S(2)}, u32[]{:S(2)}) async-start(f32[8,128,20]{1,2,0:T(8,128)} %copy.10), calls=%async_computation.2 | async-start | bytes 196608 | tf_op jit(solution)/shard_map/all_to_all | solution.py:38
